TPU v7x, 512 devices: a whole 4x8x8 slice. The times are simulated.
512 devices in a mesh: doc: 16 (over z_lo, y), ctx: 32 (over z_hi, x, core).
Axes of the slice: x: 4, y: 8, z: 8 (z_hi: 4, z_lo: 2; z = z_hi * 2 + z_lo), core: 2. Of those that a mesh axis runs over, the one named last changes fastest.
Arguments:
- queries: bfloat16 [16, 4096, 4096], P('doc', 'ctx'), may hold values from -6 to 6, as said below
- key_heads: bfloat16 [16, 4096, 512], P('doc', 'ctx'), may hold values from -6 to 6, as said below
- value_heads: bfloat16 [16, 4096, 512], P('doc', 'ctx'), may hold values from -6 to 6
- out_grad: bfloat16 [16, 4096, 4096], P('doc', 'ctx'), may hold values from -6 to 6
- log_sums: float32 [16, 32, 4096], P('doc', 'ctx'), as said below
- row_delta: float32 [16, 32, 4096], P('doc', 'ctx'), may hold values from -6 to 6
- doc_start: int32 [16], P('doc'), may hold values from 0 to 2048, as said below
- layer_input: bfloat16 [16, 4096, 8192], P('doc', 'ctx'), may hold values from -6 to 6
- hash_in: int32 [8192], replicated, may hold values from 0 to 255
- hash_out: int32 [4096], P('ctx'), may hold values from 0 to 127
- query_sketch: bfloat16 [4096, 8192], P('doc', 'ctx'), may hold values from -6 to 6
Outputs:
- doc_sketch: float32 [16, 8192], P('doc', 'ctx')
- scores: float32 [16, 4096], P(None, ('doc', 'ctx'))
Inputs may be any that keep to these rules, and one draw needn't show every extreme that they name: `queries`: drawn together with key_heads; float values. `key_heads`: drawn together with queries; float values. log_sums[e, h, i] is the log of the sum of exp(logits[i, j]) over the positions j visible to i, for the given queries and key_heads; 0 for rows before doc_start[e]. `doc_start`: some document starts at 0 and some at 2048.
All inputs are finite; a program needn't handle non-finite values.
Results may differ from a plain program's by a relative error of at most 0.024.
Values may be sent and summed in bfloat16 or wider, within the bound.
A program may use at most 128 MiB of HBM per device.

v0:
```python
import jax
import jax.numpy as jnp
from jax import lax
from jax.sharding import PartitionSpec as P

HD = 128
K1 = 128
K2 = 64


def sign_table(codes, buckets):
    levels = jnp.arange(buckets, dtype=jnp.int32)
    plus_part = (codes[..., None] == levels).astype(jnp.float32)
    minus_part = (codes[..., None] == levels + buckets).astype(jnp.float32)
    return (plus_part - minus_part).astype(jnp.bfloat16)


def local(
    queries,
    key_heads,
    value_heads,
    out_grad,
    log_sums,
    row_delta,
    doc_start,
    layer_input,
    hash_in,
    hash_out,
    query_sketch,
):
    ctx_count = lax.axis_size("ctx")
    tok_rows = queries.shape[1]
    seq_len = tok_rows * ctx_count
    local_heads = log_sums.shape[1]
    all_heads = local_heads * ctx_count
    kv_count = key_heads.shape[2] // HD
    group_size = all_heads // kv_count
    query_local = queries[0].reshape(tok_rows, all_heads, HD)
    grad_local = out_grad[0].reshape(tok_rows, all_heads, HD)
    key_local = key_heads[0].reshape(tok_rows, kv_count, HD)
    value_local = value_heads[0].reshape(tok_rows, kv_count, HD)
    query_part, grad_part = (
        lax.all_to_all(query_local, "ctx", split_axis=1, concat_axis=0, tiled=True),
        lax.all_to_all(grad_local, "ctx", split_axis=1, concat_axis=0, tiled=True),
    )
    key_all, value_all = (
        lax.all_gather(key_local, "ctx", axis=0, tiled=True),
        lax.all_gather(value_local, "ctx", axis=0, tiled=True),
    )
    first_head = lax.axis_index("ctx") * local_heads
    kv_index = (first_head + jnp.arange(local_heads, dtype=jnp.int32)) // group_size
    key_part = jnp.take(key_all, kv_index, axis=1)
    value_part = jnp.take(value_all, kv_index, axis=1)
    factor = HD ** (-0.5)
    first_pos = doc_start[0]
    log_part = log_sums[0]
    delta_part = row_delta[0]
    block_rows = min(256, seq_len)
    pieces = []
    for block_index in range(seq_len // block_rows):
        low_row = block_index * block_rows
        high_row = low_row + block_rows
        query_rows = query_part[low_row:high_row]
        grad_rows = grad_part[low_row:high_row]
        key_rows = key_part[:high_row]
        value_rows = value_part[:high_row]
        logits = (
            jnp.einsum("qhd,khd->hqk", query_rows, key_rows, preferred_element_type=jnp.float32)
            * factor
        )
        row_pos = low_row + jnp.arange(block_rows, dtype=jnp.int32)
        col_pos = jnp.arange(high_row, dtype=jnp.int32)
        visible = (col_pos[None, :] <= row_pos[:, None]) & (col_pos[None, :] >= first_pos)
        weights = jnp.where(
            visible[None], jnp.exp(logits - log_part[:, low_row:high_row, None]), 0.0
        )
        grad_weights = jnp.einsum(
            "qhd,khd->hqk", grad_rows, value_rows, preferred_element_type=jnp.float32
        )
        grad_scores = (weights * (grad_weights - delta_part[:, low_row:high_row, None])).astype(
            jnp.bfloat16
        )
        grad_query = (
            jnp.einsum("hqk,khd->qhd", grad_scores, key_rows, preferred_element_type=jnp.float32)
            * factor
        )
        pieces.append(grad_query.astype(jnp.bfloat16))
    grad_full = jnp.concatenate(pieces, axis=0)
    table_out = sign_table(hash_out.reshape(local_heads, HD), K2)
    hashed_grads = jnp.einsum(
        "shd,hdb->shb", grad_full, table_out, preferred_element_type=jnp.float32
    ).astype(jnp.bfloat16)
    table_in = sign_table(hash_in, K1)
    hashed_local = jnp.dot(layer_input[0], table_in, preferred_element_type=jnp.float32).astype(
        jnp.bfloat16
    )
    hashed_all = lax.all_gather(hashed_local, "ctx", axis=0, tiled=True)
    partial_sketch = jnp.einsum(
        "sa,shb->ab", hashed_all, hashed_grads, preferred_element_type=jnp.float32
    )
    summed = lax.psum_scatter(
        partial_sketch.astype(jnp.bfloat16), "ctx", scatter_dimension=0, tiled=True
    ).astype(jnp.float32)
    local_sketch = (summed * (seq_len * layer_input.shape[2] // K1) ** (-0.5)).reshape(1, -1)
    every_sketch = lax.all_gather(local_sketch, "doc", axis=0, tiled=True)
    partial_scores = jnp.dot(
        every_sketch, query_sketch.astype(jnp.float32).T, precision=lax.Precision.HIGHEST
    )
    scores_part = lax.psum_scatter(partial_scores, "ctx", scatter_dimension=1, tiled=True) * (
        K1 * K2
    ) ** (-0.5)
    return (local_sketch, scores_part)


def solution(mesh):
    return jax.shard_map(
        local,
        mesh=mesh,
        in_specs=(
            P("doc", "ctx", None),
            P("doc", "ctx", None),
            P("doc", "ctx", None),
            P("doc", "ctx", None),
            P("doc", "ctx", None),
            P("doc", "ctx", None),
            P("doc"),
            P("doc", "ctx", None),
            P(),
            P("ctx"),
            P("doc", "ctx"),
        ),
        out_specs=(P("doc", "ctx"), P(None, ("doc", "ctx"))),
        check_vma=False,
    )
```

profile of v0, /device:TPU:1, one launch (start us, length us, event | category | flops | bytes accessed | tf_op | source)
XLA Modules:
  0.0 599.1 jit_solution(1835054728151453104)
XLA Ops:
  7.2 1.8 copy.85
  9.1 1.7 copy.81
  10.8 2.3 copy.83
  13.1 14.4 %all-to-all-start = ((bf16[128,32,128]{0,2,1:T(8,128)(2,1)}), bf16[128,32,128]{0,2,1:T(8,128)(2,1)S(1)}, u32[]{:S(2)}, u32[]{:S(2)}) async-start(bf16[128,32,128]{0,2,1:T(8,128)(2,1)} %bitcast.752), calls=%async_computation | async-start | bytes 2097152 | tf_op jit(solution)/shard_map/all_to_all | solution.py:43
  27.6 2.5 fusion.219
  31.8 2.3 copy.87
  47.1 7.2 %all-to-all-done = bf16[128,32,128]{0,2,1:T(8,128)(2,1)S(1)} async-done(((bf16[128,32,128]{0,2,1:T(8,128)(2,1)}), bf16[128,32,128]{0,2,1:T(8,128)(2,1)S(1)}, u32[]{:S(2)}, u32[]{:S(2)}) %all-to-all-start) | async-done | bytes 1048608 | tf_op jit(solution)/shard_map/all_to_all | solution.py:43
  54.3 10.9 %all-to-all-start.1 = ((bf16[128,32,128]{0,2,1:T(8,128)(2,1)}), bf16[128,32,128]{0,2,1:T(8,128)(2,1)}, u32[]{:S(2)}, u32[]{:S(2)}) async-start(bf16[128,32,128]{0,2,1:T(8,128)(2,1)} %bitcast.751), calls=%async_computation.1 | async-start | bytes 2097152 | tf_op jit(solution)/shard_map/all_to_all | solution.py:44
  74.5 1.6 copy.84
  76.2 18.1 %all-to-all-done.1 = bf16[128,32,128]{0,2,1:T(8,128)(2,1)} async-done(((bf16[128,32,128]{0,2,1:T(8,128)(2,1)}), bf16[128,32,128]{0,2,1:T(8,128)(2,1)}, u32[]{:S(2)}, u32[]{:S(2)}) %all-to-all-start.1) | async-done | bytes 1048608 | tf_op jit(solution)/shard_map/all_to_all | solution.py:44
  94.2 2.1 fusion.271
  124.6 1.9 fusion.129
  126.5 2.5 fusion.72
  129.0 1.9 fusion.47
  131.0 2.1 fusion.42
  133.1 2.1 fusion.37
  135.2 55.8 %all-gather.7.cloned.1.call-done = bf16[4096,4,128]{0,2,1:T(8,128)(2,1)} async-done(((bf16[128,4,128]{0,2,1:T(8,128)(2,1)}), bf16[4096,4,128]{0,2,1:T(8,128)(2,1)}) %all-gather.7.cloned.1.call-update) | async-done | bytes 4194320 | tf_op jit(solution)/shard_map/all_gather | solution.py:47
  193.3 1.8 fusion.148
  195.1 2.0 fusion.190
  197.1 2.2 fusion.120
  199.3 2.3 fusion.192
  201.7 2.4 fusion.196
  204.1 2.5 fusion.110
  206.6 2.5 fusion.194
  209.1 2.7 fusion.77
  211.8 2.7 fusion.184
  214.5 2.9 fusion.80
  217.5 2.8 fusion.198
  220.3 3.3 fusion.86
  223.6 3.4 fusion.212
  227.0 3.2 fusion.186
  230.2 4.3 fusion.53
  234.5 4.0 fusion.204
  238.5 4.1 fusion.210
  242.6 4.5 fusion.206
  247.1 3.8 fusion.214
  251.0 4.6 fusion.10
  255.6 3.9 fusion.5
  259.6 2.4 fusion.17
  262.0 4.1 fusion.23
  266.1 4.9 fusion.208
  271.0 4.1 fusion.188
  275.1 4.3 fusion.200
  279.4 4.5 fusion.202
  283.9 2.2 fusion.215
  286.2 135.6 %all-reduce = bf16[128,64]{1,0:T(8,128)(2,1)S(1)} all-reduce(bf16[128,64]{1,0:T(8,128)(2,1)S(1)} %fusion.215), channel_id=2, replica_groups=mesh['doc'=16,'ctx'=32] {'ctx'}, use_global_device_ids=true, to_apply=%region_0.2.clone | all-reduce | flops 8192 | bytes 32768
  422.5 24.0 %all-gather = f32[16,1,256]{2,1,0:T(1,128)S(1)} all-gather(f32[1,1,256]{2,1,0:T(1,128)S(1)} %reshape.1028), channel_id=1, replica_groups=mesh['doc'=16,'ctx'=32] {'doc'}, dimensions={0}, use_global_device_ids=true | all-gather | bytes 17408 | tf_op jit(solution)/shard_map/all_gather | solution.py:105
  446.7 145.3 %all-reduce.1 = f32[16,256]{0,1:T(8,128)S(1)} all-reduce(f32[16,256]{0,1:T(8,128)S(1)} %fusion.252), channel_id=3, replica_groups=mesh['doc'=16,'ctx'=32] {'ctx'}, use_global_device_ids=true, to_apply=%region_1.3.clone | all-reduce | flops 4096 | bytes 32768
  (173 shorter events, 54.3 us)
Async XLA Ops:
  7.2 20.4 %copy-start = (bf16[1,128,8192]{2,1,0:T(8,128)(2,1)S(1)}, bf16[1,128,8192]{2,1,0:T(8,128)(2,1)}, u32[]{:S(2)}) copy-start(bf16[1,128,8192]{2,1,0:T(8,128)(2,1)} %param.20) | copy-start | bytes 6291460
  7.2 20.4 %copy-start.41 = (s32[8192]{0:T(1024)S(1)}, s32[8192]{0:T(1024)}, u32[]{:S(2)}) copy-start(s32[8192]{0:T(1024)} %param.21) | copy-start | bytes 98308
  7.2 116.0 %all-gather.9.cloned.1.call-start = ((), (), s32[]{:S(2)}) async-start(), calls=%async_computation.4 | async-start | bytes 4325376 | tf_op jit(solution)/shard_map/all_gather | solution.py:48
  9.1 181.9 %all-gather.7.cloned.1.call-start = ((), (), s32[]{:S(2)}) async-start(), calls=%async_computation.3 | async-start | bytes 4325376 | tf_op jit(solution)/shard_map/all_gather | solution.py:47
  13.1 41.2 %all-to-all-start = ((bf16[128,32,128]{0,2,1:T(8,128)(2,1)}), bf16[128,32,128]{0,2,1:T(8,128)(2,1)S(1)}, u32[]{:S(2)}, u32[]{:S(2)}) async-start(bf16[128,32,128]{0,2,1:T(8,128)(2,1)} %bitcast.752), calls=%async_computation | async-start | bytes 2097152 | tf_op jit(solution)/shard_map/all_to_all | solution.py:43
  27.5 256.4 %all-gather.5.cloned.1.call-start = ((), (), s32[]{:S(2)}) async-start(), calls=%async_computation.2 | async-start | bytes 1081344 | tf_op jit(solution)/shard_map/all_gather | solution.py:97
  30.1 42.2 %copy-start.24 = (f32[1,1,4096]{2,1,0:T(1,128)S(1)}, f32[1,1,4096]{2,1,0:T(1,128)}, u32[]{:S(2)}) copy-start(f32[1,1,4096]{2,1,0:T(1,128)} %param.17) | copy-start | bytes 49156
  30.1 42.9 %copy-start.25 = (f32[1,1,4096]{2,1,0:T(1,128)S(1)}, f32[1,1,4096]{2,1,0:T(1,128)}, u32[]{:S(2)}) copy-start(f32[1,1,4096]{2,1,0:T(1,128)} %param.18) | copy-start | bytes 49156
  54.3 39.9 %all-to-all-start.1 = ((bf16[128,32,128]{0,2,1:T(8,128)(2,1)}), bf16[128,32,128]{0,2,1:T(8,128)(2,1)}, u32[]{:S(2)}, u32[]{:S(2)}) async-start(bf16[128,32,128]{0,2,1:T(8,128)(2,1)} %bitcast.751), calls=%async_computation.1 | async-start | bytes 2097152 | tf_op jit(solution)/shard_map/all_to_all | solution.py:44
  74.5 26.7 %copy-start.13 = (bf16[2,128,1,128]{1,3,0,2:T(8,128)(2,1)S(1)}, bf16[2,128,1,128]{1,3,0,2:T(8,128)(2,1)}, u32[]{:S(2)}) copy-start(bf16[2,128,1,128]{1,3,0,2:T(8,128)(2,1)} %get-tuple-element.43) | copy-start | bytes 196612
  74.5 29.0 %copy-start.12 = (bf16[2,128,1,128]{1,3,0,2:T(8,128)(2,1)S(1)}, bf16[2,128,1,128]{1,3,0,2:T(8,128)(2,1)}, u32[]{:S(2)}) copy-start(bf16[2,128,1,128]{1,3,0,2:T(8,128)(2,1)} %get-tuple-element.42) | copy-start | bytes 196612
  74.5 31.3 %copy-start.11 = (bf16[2,128,1,128]{1,3,0,2:T(8,128)(2,1)S(1)}, bf16[2,128,1,128]{1,3,0,2:T(8,128)(2,1)}, u32[]{:S(2)}) copy-start(bf16[2,128,1,128]{1,3,0,2:T(8,128)(2,1)} %get-tuple-element.41) | copy-start | bytes 196612
  74.5 33.6 %copy-start.10 = (bf16[2,128,1,128]{1,3,0,2:T(8,128)(2,1)S(1)}, bf16[2,128,1,128]{1,3,0,2:T(8,128)(2,1)}, u32[]{:S(2)}) copy-start(bf16[2,128,1,128]{1,3,0,2:T(8,128)(2,1)} %get-tuple-element.40) | copy-start | bytes 196612
  74.5 37.4 %copy-start.9 = (bf16[2,128,1,128]{1,3,0,2:T(8,128)(2,1)S(1)}, bf16[2,128,1,128]{1,3,0,2:T(8,128)(2,1)}, u32[]{:S(2)}) copy-start(bf16[2,128,1,128]{1,3,0,2:T(8,128)(2,1)} %get-tuple-element.39) | copy-start | bytes 196612
  74.5 38.2 %copy-start.8 = (bf16[2,128,1,128]{1,3,0,2:T(8,128)(2,1)S(1)}, bf16[2,128,1,128]{1,3,0,2:T(8,128)(2,1)}, u32[]{:S(2)}) copy-start(bf16[2,128,1,128]{1,3,0,2:T(8,128)(2,1)} %get-tuple-element.38) | copy-start | bytes 196612
  74.5 41.2 %copy-start.7 = (bf16[2,128,1,128]{1,3,0,2:T(8,128)(2,1)S(1)}, bf16[2,128,1,128]{1,3,0,2:T(8,128)(2,1)}, u32[]{:S(2)}) copy-start(bf16[2,128,1,128]{1,3,0,2:T(8,128)(2,1)} %get-tuple-element.37) | copy-start | bytes 196612
  94.2 25.6 %copy-start.6 = (bf16[2,128,1,128]{1,3,0,2:T(8,128)(2,1)S(1)}, bf16[2,128,1,128]{1,3,0,2:T(8,128)(2,1)}, u32[]{:S(2)}) copy-start(bf16[2,128,1,128]{1,3,0,2:T(8,128)(2,1)} %get-tuple-element.33) | copy-start | bytes 196612
  123.2 5.8 copy-start.14
  123.2 5.8 copy-start.27
  126.5 4.5 copy-start.15
  126.5 4.5 copy-start.26
  129.0 4.0 copy-start.33
  135.2 59.9 %copy-start.16 = (bf16[2,128,1,128]{3,1,0,2:T(8,128)(2,1)S(1)}, bf16[2,128,1,128]{3,1,0,2:T(8,128)(2,1)}, u32[]{:S(2)}) copy-start(bf16[2,128,1,128]{3,1,0,2:T(8,128)(2,1)} %copy.88) | copy-start | bytes 196612
  199.3 7.2 %copy-start.5 = (bf16[2,128,1,128]{3,1,0,2:T(8,128)(2,1)S(1)}, bf16[2,128,1,128]{3,1,0,2:T(8,128)(2,1)}, u32[]{:S(2)}) copy-start(bf16[2,128,1,128]{3,1,0,2:T(8,128)(2,1)} %copy.100) | copy-start | bytes 196612
  211.8 5.7 copy-start.4
  223.6 3.4 copy-start.3
  230.2 4.3 copy-start.23
  230.2 4.3 copy-start.35
  238.5 4.1 copy-start.22
  238.5 4.1 copy-start.34
  247.1 3.8 copy-start.21
  247.1 3.8 copy-start.31
  250.9 4.7 copy-start.2
  250.9 4.7 copy-start.20
  251.0 4.7 copy-start.30
  251.0 4.7 copy-start.38
  251.0 4.7 copy-start.44
  259.6 2.4 copy-start.29
  259.6 2.4 copy-start.37
  259.6 2.4 copy-start.43
  262.0 4.1 copy-start.18
  262.0 4.1 copy-start.28
  262.0 4.1 copy-start.36
  262.0 4.1 copy-start.42
  275.1 4.3 copy-start.32
  279.4 4.5 copy-start.39
  279.4 4.5 copy-start.40
  279.4 167.0 %copy-start.17 = (bf16[256,256]{1,0:T(8,128)(2,1)S(1)}, bf16[256,256]{1,0:T(8,128)(2,1)}, u32[]{:S(2)}) copy-start(bf16[256,256]{1,0:T(8,128)(2,1)} %param.23) | copy-start | bytes 393220
  (2 other events, 3.4 us)
Sparse Core Ops, SparseCore 0:
  11.1 105.5 all-gather.8
  119.8 71.1 all-gather.6
  194.0 55.7 all-gather.4
where the time goes:
time: 606 us; the launch traced here: 599 us
  blocking collectives  305 us (50%)
  matrix products  106 us (17%)
  waiting for transfers between devices  81.2 us (13%)
  local copies, waits for them, and re-layouts  43.8 us (7%)
  starting transfers between devices  25.4 us (4%)
  other arithmetic  21.9 us (4%)
  between operations  16.1 us (3%)
    unnamed x2, blocking collectives  281 us
    all_gather x1, waiting for transfers between devices, local(): lax.all_gather(key_local, 'ctx', axis=0, tiled=True)  55.8 us
    dot_general x16, matrix products, local(): jnp.einsum('hqk,khd->qhd', grad_scores, key_rows, preferred_element_type=...  55.6 us
    dot_general x10, matrix products, local(): jnp.einsum('qhd,khd->hqk', query_rows, key_rows, preferred_element_type=j...  32.4 us
    all_gather x1, blocking collectives, local(): every_sketch = lax.all_gather(local_sketch, 'doc', axis=0, tiled=True)  24 us
    all_to_all x1, waiting for transfers between devices, local(): lax.all_to_all(grad_local, 'ctx', split_axis=1, concat_axis=0, tiled=True)  18.1 us
    slice x17, local copies, waits for them, and re-layouts, local(): grad_rows = grad_part[low_row:high_row]  16.9 us
    slice x17, local copies, waits for them, and re-layouts, local(): query_rows = query_part[low_row:high_row]  14.4 us
  transfers between devices with their start and end apart: 5, of which 3 were waited for; matrix products, arithmetic and copies ran while one was open for 28% of the time, Pallas kernels for 0%

commit v1 on v0

v1 whole, which is shorter than its diff:
```python
import functools

import jax
import jax.numpy as jnp
from jax import lax
from jax.experimental import pallas as pl
from jax.experimental.pallas import tpu as pltpu
from jax.sharding import PartitionSpec as P

HD = 128
K1 = 128
K2 = 64
SEQ = 4096
DIM = 8192
DOCS = 16
RANKS = 32
ROWS = 128
BLOCK = 256
PLANE = 1024
LOG2E = 1.4426950408889634
SCORE = HD**-0.5
NEG = -1e30
NT = (((1,), (1,)), ((), ()))
TN = (((0,), (0,)), ((), ()))
F32 = jnp.float32
BF16 = jnp.bfloat16


def kernel(
    q_hbm, k_hbm, v_hbm, do_hbm, lse_ref, dl_ref, start_ref, x_hbm, hin_ref, hout_ref, qs_ref,
    sketch_out, scores_out,
    qb, dob, kv, acc, xb, ld, msg, hit_own, hit, bias, part, rs1, sk_send, sk_all, part2, rs2,
    xsem, lsem, msg_ss, msg_rs, kx_ss, kx_rs, q_ss, q_rs, do_ss, do_rs, z_ss, z_rs, s_ss, s_rs,
    hi_ss, hi_rs, r1_ss, r1_rs, ag_ss, ag_rs, r2_ss, r2_rs,
):
    doc = lax.axis_index("doc")
    me = lax.axis_index("ctx")
    zz = me // 8
    xx = (me // 2) % 4
    cc = me % 2
    base = zz * 8
    in_plane = me % 8

    def remote(src, dst, ss, rs, peer):
        return pltpu.make_async_remote_copy(
            src_ref=src, dst_ref=dst, send_sem=ss, recv_sem=rs,
            device_id={"ctx": peer}, device_id_type=pl.DeviceIdType.MESH,
        )

    barrier = pltpu.get_barrier_semaphore()

    def greet(i, _):
        pl.semaphore_signal(
            barrier, inc=1, device_id={"ctx": (me + i) % RANKS},
            device_id_type=pl.DeviceIdType.MESH,
        )
        return 0

    lax.fori_loop(1, RANKS, greet, 0)

    def greet_doc(i, _):
        pl.semaphore_signal(
            barrier, inc=1, device_id={"doc": (doc + i) % DOCS},
            device_id_type=pl.DeviceIdType.MESH,
        )
        return 0

    lax.fori_loop(1, DOCS, greet_doc, 0)

    x_copy = pltpu.make_async_copy(x_hbm.at[0], xb, xsem)
    x_copy.start()
    ld[0] = lse_ref[...] * LOG2E
    ld[1] = dl_ref[...]
    ld[2] = jnp.broadcast_to(hout_ref[...].astype(F32), (32, 128))

    pl.semaphore_wait(barrier, RANKS - 1 + DOCS - 1)

    def kx(i):
        to = (in_plane + i) % 8
        lanes = pl.ds(pl.multiple_of((to // 2) * HD, HD), HD)
        rows = pl.ds(pl.multiple_of(me * ROWS, ROWS), ROWS)
        return to, (
            (k_hbm.at[0, :, lanes], kv.at[0, rows, :]),
            (v_hbm.at[0, :, lanes], kv.at[1, rows, :]),
        )

    def kx_start(i, _):
        to, pairs = kx(i)
        for src, dst in pairs:
            remote(src, dst, kx_ss, kx_rs, base + to).start()
        return 0

    lax.fori_loop(1, 8, kx_start, 0)
    for src, dst in kx(0)[1]:
        pltpu.make_async_copy(src, dst, kx_rs).start()

    own_head = (me // 8) * 2 + (me % 8) // 4
    slot = me % 4

    def msg_pair(i):
        rows = pl.ds(pl.multiple_of(i * 8, 8), 8)
        return ld.at[:, rows, :], msg.at[slot]

    def msg_each(i, go):
        src, dst = msg_pair(i)
        peer = i * 8 + own_head

        @pl.when(peer != me)
        def _():
            go(remote(src, dst, msg_ss.at[i], msg_rs.at[slot], peer))

        return src, dst, peer

    def msg_start(i, _):
        src, dst, peer = msg_each(i, lambda c: c.start())

        @pl.when(peer == me)
        def _():
            pltpu.make_async_copy(src, dst, msg_rs.at[slot]).start()

        return 0

    lax.fori_loop(0, 4, msg_start, 0)

    def qx(i):
        to = (in_plane + i) % 8
        lanes = pl.ds(pl.multiple_of(to * 512, 512), 512)
        rows = pl.ds(pl.multiple_of(cc * ROWS, ROWS), ROWS)
        return to, (q_hbm.at[0, :, lanes], qb.at[xx, rows, :]), (
            do_hbm.at[0, :, lanes],
            dob.at[xx, rows, :],
        )

    def qx_copy(i):
        to, a, b = qx(i)
        return (
            remote(*a, q_ss.at[i], q_rs.at[xx], base + to),
            remote(*b, do_ss.at[i], do_rs.at[xx], base + to),
        )

    for src, dst, sem in ((*qx(0)[1], q_rs.at[xx]), (*qx(0)[2], do_rs.at[xx])):
        pltpu.make_async_copy(src, dst, sem).start()

    def qx_order(n):
        near = jnp.where(n < 3, 2, jnp.where(n < 5, 6, 4))
        other = near + ((n + 1) % 2) * (1 - 2 * cc)
        return jnp.where(n == 0, (1 - 2 * cc) % 8, other % 8)

    def qx_start(n, _):
        a, b = qx_copy(qx_order(n))
        a.start()
        b.start()
        return 0

    lax.fori_loop(0, 7, qx_start, 0)

    x_copy.wait()
    bucket_of = lax.broadcasted_iota(jnp.int32, (K1, 1024), 0)

    def hash_step(j, total):
        cols = pl.ds(pl.multiple_of(j * 1024, 1024), 1024)
        codes = hin_ref[:, cols]
        low = codes < K1
        bucket = jnp.where(low, codes, codes - K1)
        sign = jnp.where(low, 1.0, -1.0)
        table = jnp.where(bucket_of == bucket, sign, 0.0).astype(BF16)
        return total + lax.dot_general(table, xb[:, cols], NT, preferred_element_type=F32)

    hit_own[...] = lax.fori_loop(0, DIM // 1024, hash_step, jnp.zeros((K1, ROWS), F32)).astype(BF16)

    hit_lanes = pl.ds(pl.multiple_of(in_plane * ROWS, ROWS), ROWS)

    def hit_copy(i):
        return remote(hit_own, hit.at[:, hit_lanes], hi_ss.at[i], hi_rs, base + (in_plane + i) % 8)

    def hit_start(i, _):
        hit_copy(i).start()
        return 0

    lax.fori_loop(1, 8, hit_start, 0)
    pltpu.make_async_copy(hit_own, hit.at[:, hit_lanes], hi_rs).start()

    bias[...] = jnp.where(
        lax.broadcasted_iota(jnp.int32, (SEQ, HD), 0) >= start_ref[0], 0.0, NEG
    ).astype(F32)
    acc[...] = jnp.zeros_like(acc)

    own_rows = pl.ds(pl.multiple_of(zz * PLANE, PLANE), PLANE)
    pltpu.make_async_copy(kv.at[:, own_rows, :], kv.at[:, own_rows, :], kx_rs).wait()

    def half(plane, core):
        return kv.at[:, pl.ds(pl.multiple_of(plane * PLANE + core * 512, 512), 512), :]

    def z_copy(plane, to, s):
        return remote(half(plane, cc), half(plane, cc), z_ss.at[s], z_rs.at[plane], to * 8 + in_plane)

    def s_copy(plane):
        return remote(
            half(plane, cc), half(plane, cc), s_ss.at[plane], s_rs.at[plane], me + 1 - 2 * cc
        )

    @pl.when(zz < 3)
    def _():
        z_copy(zz, zz + 1, 0).start()

    @pl.when(zz == 0)
    def _():
        z_copy(0, 3, 1).start()

    def z_arrive(plane):
        pltpu.make_async_copy(half(plane, cc), half(plane, cc), z_rs.at[plane]).wait()
        s_copy(plane).start()

    def s_arrive(plane):
        pltpu.make_async_copy(
            half(plane, 1 - cc), half(plane, 1 - cc), s_rs.at[plane]
        ).wait()

    def front(rb, h, kk, vv):
        head = slice(h * HD, (h + 1) * HD)
        s = lax.dot_general(kk, qb[rb, :, head], NT, preferred_element_type=F32)
        gw = lax.dot_general(vv, dob[rb, :, head], NT, preferred_element_type=F32)
        return s, gw

    def back(rb, h, kk, low, s, gw, diagonal):
        count = kk.shape[0]
        lse = jnp.concatenate(
            [msg[h, 0, pl.ds(2 * rb, 1), :], msg[h, 0, pl.ds(2 * rb + 1, 1), :]], axis=1
        )
        delta = jnp.concatenate(
            [msg[h, 1, pl.ds(2 * rb, 1), :], msg[h, 1, pl.ds(2 * rb + 1, 1), :]], axis=1
        )
        x = s * (SCORE * LOG2E) - lse + jnp.concatenate([low, low], axis=1)
        p = jnp.exp2(x)
        if diagonal:
            seen = lax.broadcasted_iota(jnp.int32, (BLOCK, BLOCK), 0) <= lax.broadcasted_iota(
                jnp.int32, (BLOCK, BLOCK), 1
            )
            last = jnp.where(seen, p[count - BLOCK :], 0.0)
            p = last if count == BLOCK else jnp.concatenate([p[: count - BLOCK], last], axis=0)
        ds = (p * (gw - delta)).astype(BF16)
        r = lax.dot_general(kk, ds, TN, preferred_element_type=F32)
        rows = pl.ds(pl.multiple_of((rb * 4 + h) * HD, HD), HD)
        acc[rows, :] += r

    def heads(rb, lo, count, diagonal):
        keys = pl.ds(pl.multiple_of(lo, BLOCK), count)
        kk = kv[0, keys, :]
        vv = kv[1, keys, :]
        low = bias[keys, :]
        now = front(rb, 0, kk, vv)
        for h in range(4):
            later = front(rb, h + 1, kk, vv) if h < 3 else None
            back(rb, h, kk, low, *now, diagonal)
            now = later

    def order(i):
        return (xx + jnp.where(i == 2, 3, jnp.where(i == 3, 2, i))) % 4

    def diag_step(i, _):
        rb = order(i)
        rows = qb.at[rb]
        pltpu.make_async_copy(rows, rows, q_rs.at[rb]).wait()
        rows = dob.at[rb]
        pltpu.make_async_copy(rows, rows, do_rs.at[rb]).wait()
        for r in range(4):

            @pl.when(rb == r)
            def _():
                heads(r, zz * PLANE, (r + 1) * BLOCK, True)

        return 0

    def plane_steps(plane, first, last):
        def step(i, _):
            heads(order(i), plane * PLANE, PLANE, False)
            return 0

        lax.fori_loop(first, last, step, 0)

    def msg_wait(i, _):
        pltpu.make_async_copy(msg.at[i], msg.at[i], msg_rs.at[i]).wait()
        return 0

    lax.fori_loop(0, 4, msg_wait, 0)

    lax.fori_loop(0, 3, diag_step, 0)

    @pl.when(zz >= 1)
    def _():
        z_arrive(zz - 1)

        @pl.when(zz < 3)
        def _():
            z_copy(zz - 1, zz + 1, 1).start()

    @pl.when(zz == 3)
    def _():
        z_arrive(0)

    @pl.when(zz >= 1)
    def _():
        s_arrive(zz - 1)
        plane_steps(zz - 1, 0, 3)

    @pl.when(zz == 3)
    def _():
        s_arrive(0)
        plane_steps(0, 0, 3)

    lax.fori_loop(3, 4, diag_step, 0)

    @pl.when(zz >= 1)
    def _():
        plane_steps(zz - 1, 3, 4)

    @pl.when(zz == 3)
    def _():
        z_arrive(1)
        plane_steps(0, 3, 4)
        s_arrive(1)
        plane_steps(1, 0, 4)

    @pl.when(zz == 2)
    def _():
        z_arrive(0)
        s_arrive(0)
        plane_steps(0, 0, 4)

    pltpu.make_async_copy(hit, hit, hi_rs).wait()
    feature_bucket = lax.broadcasted_iota(jnp.int32, (K2, HD), 0).astype(F32)
    pieces = []
    for h in range(4):
        codes = msg[h, 2, 0:1, :]
        low = codes < K2
        bucket = jnp.where(low, codes, codes - K2)
        sign = jnp.where(low, 1.0, -1.0)
        pieces.append(jnp.where(feature_bucket == bucket, sign, 0.0).astype(BF16))
    table_out = jnp.concatenate(pieces, axis=1)
    total = jnp.zeros((K1, 2 * K2), F32)
    for rb in range(4):
        gq = (acc[rb * 512 : (rb + 1) * 512, :] * SCORE).astype(BF16)
        hg = jnp.dot(table_out, gq, preferred_element_type=F32)
        high = hg.astype(BF16)
        rest = (hg - high.astype(F32)).astype(BF16)
        both = jnp.concatenate([high, rest], axis=0)
        total += lax.dot_general(
            hit[:, rb * BLOCK : (rb + 1) * BLOCK], both, NT, preferred_element_type=F32
        )
    part[...] = total

    def r1_start(i, _):
        to = (me + i) % RANKS
        rows = pl.ds(pl.multiple_of((to // 2) * 8, 8), 8)
        remote(part.at[rows, :], rs1.at[me], r1_ss, r1_rs, to).start()
        return 0

    lax.fori_loop(1, RANKS, r1_start, 0)
    mine = pl.ds(pl.multiple_of((me // 2) * 8, 8), 8)
    pltpu.make_async_copy(part.at[mine, :], rs1.at[me], r1_rs).start()
    pltpu.make_async_copy(rs1, rs1, r1_rs).wait()
    summed = jnp.sum(rs1[...], axis=0)
    summed = (summed + pltpu.roll(summed, K2, 1)) * (SEQ * DIM // K1) ** -0.5
    summed = jnp.where(cc == 0, summed, pltpu.roll(summed, 4, 0))
    left = lax.broadcasted_iota(jnp.int32, (1, HD), 1) < K2
    first = jnp.where(left, summed[0:1, :], summed[1:2, :])
    second = jnp.where(left, summed[2:3, :], summed[3:4, :])
    sketch_out[...] = jnp.concatenate([first, second], axis=1)
    sk_send[...] = jnp.concatenate([first, second, jnp.zeros((6, HD), F32)], axis=0)

    def ag_copy(i):
        return pltpu.make_async_remote_copy(
            src_ref=sk_send, dst_ref=sk_all.at[doc], send_sem=ag_ss, recv_sem=ag_rs,
            device_id={"doc": (doc + i) % DOCS}, device_id_type=pl.DeviceIdType.MESH,
        )

    def ag_start(i, _):
        ag_copy(i).start()
        return 0

    lax.fori_loop(1, DOCS, ag_start, 0)
    pltpu.make_async_copy(sk_send, sk_all.at[doc], ag_rs).start()
    pltpu.make_async_copy(sk_all, sk_all, ag_rs).wait()

    flat = sk_all[...].reshape(DOCS * 8, HD)
    stored = qs_ref[...].astype(F32)
    high = lax.Precision.HIGHEST
    even = lax.dot_general(stored[:, :HD], flat, NT, precision=high, preferred_element_type=F32)
    odd = lax.dot_general(stored[:, HD:], flat, NT, precision=high, preferred_element_type=F32)
    part2[...] = even + pltpu.roll(odd, HD - 1, 1)

    def r2_start(i, _):
        to = (me + i) % RANKS
        rows = pl.ds(pl.multiple_of(to * 8, 8), 8)
        remote(part2.at[rows, :], rs2.at[me], r2_ss, r2_rs, to).start()
        return 0

    lax.fori_loop(1, RANKS, r2_start, 0)
    mine = pl.ds(pl.multiple_of(me * 8, 8), 8)
    pltpu.make_async_copy(part2.at[mine, :], rs2.at[me], r2_rs).start()
    pltpu.make_async_copy(rs2, rs2, r2_rs).wait()
    totals = jnp.sum(rs2[...], axis=0) * (K1 * K2) ** -0.5
    pick = (
        lax.broadcasted_iota(jnp.int32, (DOCS, HD), 1)
        == 8 * lax.broadcasted_iota(jnp.int32, (DOCS, HD), 0)
    ).astype(F32)
    scores_out[...] = lax.dot_general(
        pick, totals, NT, precision=high, preferred_element_type=F32
    )

    for src in (kv.at[:, 0:896, :],):
        pltpu.make_async_copy(src, src, kx_ss).wait()

    def msg_done(i, _):
        msg_each(i, lambda c: c.wait_send())
        return 0

    lax.fori_loop(0, 4, msg_done, 0)

    def qx_done(i, _):
        a, b = qx_copy(i)
        a.wait_send()
        b.wait_send()
        hit_copy(i).wait_send()
        return 0

    lax.fori_loop(1, 8, qx_done, 0)

    @pl.when(zz < 3)
    def _():
        z_copy(zz, zz + 1, 0).wait_send()

    @pl.when(zz == 0)
    def _():
        z_copy(0, 3, 1).wait_send()

    @pl.when((zz == 1) | (zz == 2))
    def _():
        z_copy(zz - 1, zz + 1, 1).wait_send()

    def s_done(i, _):
        s_copy(i).wait_send()
        return 0

    lax.fori_loop(0, zz, s_done, 0)
    pltpu.make_async_copy(rs1.at[1:], rs1.at[1:], r1_ss).wait()
    pltpu.make_async_copy(sk_all.at[1:], sk_all.at[1:], ag_ss).wait()
    pltpu.make_async_copy(rs2.at[1:], rs2.at[1:], r2_ss).wait()


def local(
    queries, key_heads, value_heads, out_grad, log_sums, row_delta, doc_start,
    layer_input, hash_in, hash_out, query_sketch,
):
    hbm = pl.BlockSpec(memory_space=pl.ANY)
    vmem = pl.BlockSpec(memory_space=pltpu.VMEM)
    smem = pl.BlockSpec(memory_space=pltpu.SMEM)
    dma = pltpu.SemaphoreType.DMA
    return pl.pallas_call(
        kernel,
        out_shape=(
            jax.ShapeDtypeStruct((1, 256), F32),
            jax.ShapeDtypeStruct((DOCS, 8), F32),
        ),
        in_specs=[hbm, hbm, hbm, hbm, vmem, vmem, smem, hbm, vmem, vmem, vmem],
        out_specs=(vmem, vmem),
        scratch_shapes=[
            pltpu.VMEM((4, BLOCK, 512), BF16),
            pltpu.VMEM((4, BLOCK, 512), BF16),
            pltpu.VMEM((2, SEQ, HD), BF16),
            pltpu.VMEM((2048, BLOCK), F32),
            pltpu.VMEM((ROWS, DIM), BF16),
            pltpu.VMEM((3, 32, HD), F32),
            pltpu.VMEM((4, 3, 8, HD), F32),
            pltpu.VMEM((K1, ROWS), BF16),
            pltpu.VMEM((K1, PLANE), BF16),
            pltpu.VMEM((SEQ, HD), F32),
            pltpu.VMEM((K1, 2 * K2), F32),
            pltpu.VMEM((RANKS, 8, HD), F32),
            pltpu.VMEM((8, HD), F32),
            pltpu.VMEM((DOCS, 8, HD), F32),
            pltpu.VMEM((256, HD), F32),
            pltpu.VMEM((RANKS, 8, HD), F32),
            dma, dma,
            dma((4,)), dma((4,)),
            dma, dma,
            dma((8,)), dma((4,)), dma((8,)), dma((4,)),
            dma((2,)), dma((4,)), dma((4,)), dma((4,)),
            dma((8,)), dma,
            dma, dma, dma, dma, dma, dma,
        ],
        compiler_params=pltpu.CompilerParams(
            collective_id=0, has_side_effects=True, vmem_limit_bytes=56 * 2**20
        ),
    )(
        queries, key_heads, value_heads, out_grad,
        log_sums.reshape(32, 128), row_delta.reshape(32, 128), doc_start, layer_input,
        hash_in.reshape(1, DIM), hash_out.reshape(1, HD), query_sketch,
    )


def solution(mesh):
    return jax.shard_map(
        local,
        mesh=mesh,
        in_specs=(
            P("doc", "ctx", None),
            P("doc", "ctx", None),
            P("doc", "ctx", None),
            P("doc", "ctx", None),
            P("doc", "ctx", None),
            P("doc", "ctx", None),
            P("doc"),
            P("doc", "ctx", None),
            P(),
            P("ctx"),
            P("doc", "ctx"),
        ),
        out_specs=(P("doc", "ctx"), P(None, ("doc", "ctx"))),
        check_vma=False,
    )
```

time: 606 us -> 94 us (0.16); the launches traced: 599 us -> 93.8 us
  blocking collectives: 305 us -> 0 us
  matrix products: 106 us -> 0 us
  Pallas kernels: 0 us -> 89.9 us
  waiting for transfers between devices: 81.2 us -> 0 us
  local copies, waits for them, and re-layouts: 43.8 us -> 2.57 us
  starting transfers between devices: 25.4 us -> 0 us
  other arithmetic: 21.9 us -> 0 us
  between operations: 16.1 us -> 1.29 us
    unnamed x2 -> x0, blocking collectives: 281 us -> none
    dot_general x35 -> x0, matrix products: 106 us -> none  [the longest x16 55.6 us: local(): jnp.einsum('hqk,khd->qhd', grad_scores, key_rows, preferred_element_type=...]
    pallas_call x0 -> x1, Pallas kernels: none -> 89.9 us  [local(): pl.pallas_call(kernel, out_shape=(jax.ShapeDtypeStruct((1, 256), F32), ja...]
    all_gather x3 -> x0, waiting for transfers between devices: 55.8 us -> none  [the longest x1 55.8 us: local(): lax.all_gather(key_local, 'ctx', axis=0, tiled=True)]
    slice x36 -> x0, local copies, waits for them, and re-layouts: 32.6 us -> none  [the longest x17 16.9 us: local(): grad_rows = grad_part[low_row:high_row]]
    all_to_all x2 -> x0, waiting for transfers between devices: 25.3 us -> none  [the longest x1 18.1 us: local(): lax.all_to_all(grad_local, 'ctx', split_axis=1, concat_axis=0, tiled=True)]
    all_to_all x2 -> x0, starting transfers between devices: 25.3 us -> none  [the longest x1 14.4 us: local(): lax.all_to_all(query_local, 'ctx', split_axis=1, concat_axis=0, tiled=True)]
    all_gather x1 -> x0, blocking collectives: 24 us -> none  [local(): every_sketch = lax.all_gather(local_sketch, 'doc', axis=0, tiled=True)]
  transfers between devices with their start and end apart: 5 -> 0, of which waited for: 3 -> 0; matrix products, arithmetic and copies ran while one was open for 28% -> 0% of each run, Pallas kernels for 0% -> 0%
where the time goes in v1:
time: 94 us; the launch traced here: 93.8 us
  Pallas kernels  89.9 us (96%)
  local copies, waits for them, and re-layouts  2.57 us (3%)
  between operations  1.29 us (1%)
    pallas_call x1, Pallas kernels, local(): pl.pallas_call(kernel, out_shape=(jax.ShapeDtypeStruct((1, 256), F32), ja...  89.9 us

profile of v1, /device:TPU:1, one launch (start us, length us, event | category | flops | bytes accessed | tf_op | source)
XLA Modules:
  0.0 93.8 jit_solution(3418485541580936463)
XLA Ops:
  1.3 89.9 %shard_map.122 = (f32[1,256]{1,0:T(1,128)}, f32[16,8]{1,0:T(8,128)}) custom-call(bf16[1,128,4096]{2,1,0:T(8,128)(2,1)} %q_hbm.1, bf16[1,128,512]{2,1,0:T(8,128)(2,1)} %k_hbm.1, bf16[1,128,512]{2,1,0:T(8,128)(2,1)} %v_hbm.1, bf16[1,128,4096]{2,1,0:T(8,128)(2,1)} %do_hbm.1, f32[32,128]{1,0:T(8,128)} %bitcast.5, f32[32,128]{1,0:T(8,128)} %bitcast.6, ...), custom_call_target="tpu_custom_call" | custom-call | tf_op jit(solution)/shard_map/pallas_call | solution.py:459
  91.2 1.4 %copy.13 = f32[16,8]{0,1:T(8,128)} copy(f32[16,8]{1,0:T(8,128)} %get-tuple-element.3) | data formatting | bytes 1024 | tf_op jit(solution)/shard_map/pallas_call | solution.py:459
  92.5 1.2 %copy.16 = f32[1,256]{1,0:T(1,128)} copy(f32[1,256]{1,0:T(1,128)} %get-tuple-element.6) | data formatting | bytes 2048

commit v2 on v1

v2 whole, which is shorter than its diff:
```python
import functools

import jax
import jax.numpy as jnp
from jax import lax
from jax.experimental import pallas as pl
from jax.experimental.pallas import tpu as pltpu
from jax.sharding import PartitionSpec as P

HD = 128
K1 = 128
K2 = 64
SEQ = 4096
DIM = 8192
DOCS = 16
RANKS = 32
ROWS = 128
BLOCK = 256
PLANE = 1024
LOG2E = 1.4426950408889634
SCORE = HD**-0.5
NEG = -1e30
NT = (((1,), (1,)), ((), ()))
TN = (((0,), (0,)), ((), ()))
F32 = jnp.float32
BF16 = jnp.bfloat16


def wrap(value, count):
    return jnp.where(value >= count, value - count, value)


def kernel(
    q_hbm, k_hbm, v_hbm, do_hbm, lse_ref, dl_ref, start_ref, x_hbm, hin_ref, hout_ref, qs_ref,
    sketch_out, scores_out,
    qd, kv, acc, xb, ld, msg, hit_own, hit, bias, part, rs1, sk_send, sk_all, part2, rs2,
    xsem, msg_ss, msg_rs, kx_ss, kx_rs, q_ss, q_rs, z_ss, z_rs, s_ss, s_rs,
    hi_ss, hi_rs, hs_ss, hs_rs, r1_ss, r1_rs, ag_ss, ag_rs, r2_ss, r2_rs,
):
    doc = lax.axis_index("doc")
    me = lax.axis_index("ctx")
    zz = me // 8
    in_plane = me - 8 * zz
    xx = in_plane // 2
    cc = in_plane - 2 * xx
    base = zz * 8
    sibling = me + 1 - 2 * cc

    def remote(src, dst, ss, rs, peer):
        return pltpu.make_async_remote_copy(
            src_ref=src, dst_ref=dst, send_sem=ss, recv_sem=rs,
            device_id={"ctx": peer}, device_id_type=pl.DeviceIdType.MESH,
        )

    def done(ref, sem):
        pltpu.make_async_copy(ref, ref, sem).wait()

    barrier = pltpu.get_barrier_semaphore()
    for i in range(1, RANKS):
        pl.semaphore_signal(
            barrier, inc=1, device_id={"ctx": wrap(me + i, RANKS)},
            device_id_type=pl.DeviceIdType.MESH,
        )
    for i in range(1, DOCS):
        pl.semaphore_signal(
            barrier, inc=1, device_id={"doc": wrap(doc + i, DOCS)},
            device_id_type=pl.DeviceIdType.MESH,
        )
    x_copy = pltpu.make_async_copy(x_hbm.at[0], xb, xsem)
    x_copy.start()
    ld[0] = lse_ref[...] * LOG2E
    ld[1] = dl_ref[...]
    ld[2] = jnp.broadcast_to(hout_ref[...].astype(F32), (32, 128))
    pl.semaphore_wait(barrier, RANKS - 1 + DOCS - 1)

    def half(plane, core):
        return kv.at[:, pl.ds(plane * 4, 4), core]

    for dx in (1, 3, 2, 0):
        to = wrap(xx + dx, 4)
        lanes = pl.ds(pl.multiple_of(to * HD, HD), HD)
        for n, src in enumerate((k_hbm, v_hbm)):
            src = src.at[0, :, lanes]
            dst = kv.at[n, zz * 4 + xx, cc]
            if dx == 0:
                pltpu.make_async_copy(src, dst, kx_rs).start()
            else:
                remote(src, dst, kx_ss, kx_rs, base + 2 * to + cc).start()

    def z_each(go):
        @pl.when(zz < 3)
        def _():
            go(zz + 1, 0)

        @pl.when(zz == 0)
        def _():
            go(3, 1)

    def z_first(to, s):
        lanes = pl.ds(pl.multiple_of(xx * HD, HD), HD)
        for n, src in enumerate((k_hbm, v_hbm)):
            dst = kv.at[n, zz * 4 + xx, cc]
            remote(src.at[0, :, lanes], dst, z_ss.at[s], z_rs.at[zz], to * 8 + in_plane).start()

    z_each(z_first)

    rows = pl.ds(pl.multiple_of(cc * ROWS, ROWS), ROWS)

    def q_send(slot, dx, other):
        to = 2 * wrap(xx + dx, 4) + (1 - cc if other else cc)
        lanes = pl.ds(pl.multiple_of(to * 512, 512), 512)
        for n, src in enumerate((q_hbm, do_hbm)):
            src = src.at[0, :, lanes]
            dst = qd.at[n, xx, rows, :]
            if slot == 7:
                pltpu.make_async_copy(src, dst, q_rs.at[xx]).start()
            else:
                remote(src, dst, q_ss.at[slot], q_rs.at[xx], base + to).start()

    def q_left(slot):
        done(qd.at[:, 0, 0:ROWS, :], q_ss.at[slot])

    for slot, dx, other in ((0, 0, 1), (1, 1, 0), (2, 3, 0), (3, 1, 1), (4, 3, 1), (7, 0, 0)):
        q_send(slot, dx, other)

    own_head = zz * 2 + in_plane // 4
    head_slot = in_plane - 4 * (in_plane // 4)

    def msg_each(i, go):
        src, dst = ld.at[:, i * 8 : i * 8 + 8, :], msg.at[head_slot]
        peer = i * 8 + own_head

        @pl.when(peer != me)
        def _():
            go(remote(src, dst, msg_ss.at[i], msg_rs.at[head_slot], peer))

        return src, dst, peer

    for i in range(4):
        src, dst, peer = msg_each(i, lambda c: c.start())

        @pl.when(peer == me)
        def _():
            pltpu.make_async_copy(src, dst, msg_rs.at[head_slot]).start()

    def s_copy(plane):
        return remote(half(plane, cc), half(plane, cc), s_ss.at[plane], s_rs.at[plane], sibling)

    def z_block(dx, to, s):
        block = kv.at[:, zz * 4 + wrap(xx + dx, 4), cc]
        return remote(block, block, z_ss.at[s], z_rs.at[zz], to * 8 + in_plane)

    def z_send(to, s):
        for dx in (1, 3, 2):
            z_block(dx, to, s).start()

    done(half(zz, cc), kx_rs)
    z_each(z_send)
    s_copy(zz).start()

    def z_whole(plane, to, s):
        return remote(half(plane, cc), half(plane, cc), z_ss.at[s], z_rs.at[plane], to * 8 + in_plane)

    def z_arrive(plane):
        done(half(plane, cc), z_rs.at[plane])
        s_copy(plane).start()

    def s_arrive(plane):
        done(half(plane, 1 - cc), s_rs.at[plane])

    bias[...] = jnp.where(
        lax.broadcasted_iota(jnp.int32, (SEQ, HD), 0) >= start_ref[0], 0.0, NEG
    ).astype(F32)
    acc[...] = jnp.zeros_like(acc)

    x_copy.wait()
    bucket_of = lax.broadcasted_iota(jnp.int32, (K1, 1024), 0)

    def hash_step(j, total):
        cols = pl.ds(pl.multiple_of(j * 1024, 1024), 1024)
        codes = hin_ref[:, cols]
        low = codes < K1
        bucket = jnp.where(low, codes, codes - K1)
        sign = jnp.where(low, 1.0, -1.0)
        table = jnp.where(bucket_of == bucket, sign, 0.0).astype(BF16)
        return total + lax.dot_general(table, xb[:, cols], NT, preferred_element_type=F32)

    hit_own[...] = lax.fori_loop(0, DIM // 1024, hash_step, jnp.zeros((K1, ROWS), F32)).astype(BF16)

    def hit_copy(dx):
        to = base + 2 * wrap(xx + dx, 4) + cc
        return remote(hit_own, hit.at[xx, cc], hi_ss.at[dx], hi_rs, to)

    def hit_side():
        return remote(hit.at[:, cc], hit.at[:, cc], hs_ss, hs_rs, sibling)

    def front(rb, h, kk, vv):
        head = slice(h * HD, (h + 1) * HD)
        s = lax.dot_general(kk, qd[0, rb, :, head], NT, preferred_element_type=F32)
        gw = lax.dot_general(vv, qd[1, rb, :, head], NT, preferred_element_type=F32)
        return s, gw

    def back(rb, h, kk, low, s, gw, diagonal):
        count = kk.shape[0]
        lse = jnp.concatenate(
            [msg[h, 0, pl.ds(2 * rb, 1), :], msg[h, 0, pl.ds(2 * rb + 1, 1), :]], axis=1
        )
        delta = jnp.concatenate(
            [msg[h, 1, pl.ds(2 * rb, 1), :], msg[h, 1, pl.ds(2 * rb + 1, 1), :]], axis=1
        )
        x = s * (SCORE * LOG2E) - lse + jnp.concatenate([low, low], axis=1)
        p = jnp.exp2(x)
        if diagonal:
            seen = lax.broadcasted_iota(jnp.int32, (BLOCK, BLOCK), 0) <= lax.broadcasted_iota(
                jnp.int32, (BLOCK, BLOCK), 1
            )
            last = jnp.where(seen, p[count - BLOCK :], 0.0)
            p = last if count == BLOCK else jnp.concatenate([p[: count - BLOCK], last], axis=0)
        ds = (p * (gw - delta)).astype(BF16)
        r = lax.dot_general(kk, ds, TN, preferred_element_type=F32)
        rows = pl.ds(pl.multiple_of((rb * 4 + h) * HD, HD), HD)
        acc[rows, :] += r

    def heads(rb, plane, chips, diagonal):
        count = chips * BLOCK
        blocks = pl.ds(plane * 4, chips)
        kk = kv[0, blocks].reshape(count, HD)
        vv = kv[1, blocks].reshape(count, HD)
        low = bias[pl.ds(pl.multiple_of(plane * PLANE, PLANE), count), :]
        now = front(rb, 0, kk, vv)
        for h in range(4):
            later = front(rb, h + 1, kk, vv) if h < 3 else None
            back(rb, h, kk, low, *now, diagonal)
            now = later

    def order(i):
        return wrap(xx + jnp.where(i == 2, 3, jnp.where(i == 3, 2, i)), 4)

    def diag_step(i, _):
        rb = order(i)
        done(qd.at[:, rb], q_rs.at[rb])
        for r in range(4):

            @pl.when(rb == r)
            def _():
                heads(r, zz, r + 1, True)

        return 0

    def plane_steps(plane, chips, first, last):
        def step(i, _):
            heads(order(i), plane, chips, False)
            return 0

        lax.fori_loop(first, last, step, 0)

    for i in range(4):
        done(msg.at[i], msg_rs.at[i])
    s_arrive(zz)

    lax.fori_loop(0, 1, diag_step, 0)

    @pl.when(zz == 1)
    def _():
        done(half(0, 0), z_ss.at[0])
        z_whole(1, 3, 0).start()

    for slot in (1, 2, 3, 4):
        q_left(slot)
    q_send(5, 2, 0)
    q_send(6, 2, 1)
    lax.fori_loop(1, 3, diag_step, 0)

    @pl.when(zz >= 1)
    def _():
        z_arrive(zz - 1)

    @pl.when(zz == 1)
    def _():
        z_whole(0, 2, 1).start()

    @pl.when(zz == 3)
    def _():
        z_arrive(0)

    @pl.when(zz >= 1)
    def _():
        s_arrive(zz - 1)
        plane_steps(zz - 1, 4, 0, 3)

    @pl.when(zz == 3)
    def _():
        s_arrive(0)
        plane_steps(0, 4, 0, 3)

    lax.fori_loop(3, 4, diag_step, 0)
    for dx in range(1, 4):
        hit_copy(dx).start()
    pltpu.make_async_copy(hit_own, hit.at[xx, cc], hi_rs).start()

    @pl.when(zz >= 1)
    def _():
        plane_steps(zz - 1, 4, 3, 4)

    @pl.when(zz == 3)
    def _():
        z_arrive(1)
        plane_steps(0, 4, 3, 4)

    done(hit.at[:, cc], hi_rs)
    hit_side().start()

    @pl.when(zz == 3)
    def _():
        s_arrive(1)
        plane_steps(1, 4, 0, 4)

    @pl.when(zz == 2)
    def _():
        z_arrive(0)
        s_arrive(0)
        plane_steps(0, 4, 0, 4)

    done(hit.at[:, 1 - cc], hs_rs)
    feature_bucket = lax.broadcasted_iota(jnp.int32, (K2, HD), 0).astype(F32)
    pieces = []
    for h in range(4):
        codes = msg[h, 2, 0:1, :]
        low = codes < K2
        bucket = jnp.where(low, codes, codes - K2)
        sign = jnp.where(low, 1.0, -1.0)
        pieces.append(jnp.where(feature_bucket == bucket, sign, 0.0).astype(BF16))
    table_out = jnp.concatenate(pieces, axis=1)
    total = jnp.zeros((K1, 2 * K2), F32)
    for rb in range(4):
        gq = (acc[rb * 512 : (rb + 1) * 512, :] * SCORE).astype(BF16)
        hg = jnp.dot(table_out, gq, preferred_element_type=F32)
        high = hg.astype(BF16)
        rest = (hg - high.astype(F32)).astype(BF16)
        both = jnp.concatenate([high, rest], axis=0)
        total += lax.dot_general(
            jnp.concatenate([hit[rb, 0], hit[rb, 1]], axis=1), both, NT, preferred_element_type=F32
        )
    part[...] = total

    for i in range(1, RANKS):
        to = wrap(me + i, RANKS)
        rows = pl.ds(pl.multiple_of((to // 2) * 8, 8), 8)
        remote(part.at[rows, :], rs1.at[me], r1_ss, r1_rs, to).start()
    mine = pl.ds(pl.multiple_of((me // 2) * 8, 8), 8)
    pltpu.make_async_copy(part.at[mine, :], rs1.at[me], r1_rs).start()
    pltpu.make_async_copy(rs1, rs1, r1_rs).wait()
    summed = jnp.sum(rs1[...], axis=0)
    summed = (summed + pltpu.roll(summed, K2, 1)) * (SEQ * DIM // K1) ** -0.5
    summed = jnp.where(cc == 0, summed, pltpu.roll(summed, 4, 0))
    left = lax.broadcasted_iota(jnp.int32, (1, HD), 1) < K2
    first = jnp.where(left, summed[0:1, :], summed[1:2, :])
    second = jnp.where(left, summed[2:3, :], summed[3:4, :])
    sketch_out[...] = jnp.concatenate([first, second], axis=1)
    sk_send[...] = jnp.concatenate([first, second, jnp.zeros((6, HD), F32)], axis=0)

    for i in range(1, DOCS):
        pltpu.make_async_remote_copy(
            src_ref=sk_send, dst_ref=sk_all.at[doc], send_sem=ag_ss, recv_sem=ag_rs,
            device_id={"doc": wrap(doc + i, DOCS)}, device_id_type=pl.DeviceIdType.MESH,
        ).start()
    pltpu.make_async_copy(sk_send, sk_all.at[doc], ag_rs).start()
    pltpu.make_async_copy(sk_all, sk_all, ag_rs).wait()

    flat = sk_all[...].reshape(DOCS * 8, HD)
    stored = qs_ref[...].astype(F32)
    high = lax.Precision.HIGHEST
    even = lax.dot_general(stored[:, :HD], flat, NT, precision=high, preferred_element_type=F32)
    odd = lax.dot_general(stored[:, HD:], flat, NT, precision=high, preferred_element_type=F32)
    part2[...] = even + pltpu.roll(odd, HD - 1, 1)

    for i in range(1, RANKS):
        to = wrap(me + i, RANKS)
        rows = pl.ds(pl.multiple_of(to * 8, 8), 8)
        remote(part2.at[rows, :], rs2.at[me], r2_ss, r2_rs, to).start()
    mine = pl.ds(pl.multiple_of(me * 8, 8), 8)
    pltpu.make_async_copy(part2.at[mine, :], rs2.at[me], r2_rs).start()
    pltpu.make_async_copy(rs2, rs2, r2_rs).wait()
    totals = jnp.sum(rs2[...], axis=0) * (K1 * K2) ** -0.5
    pick = (
        lax.broadcasted_iota(jnp.int32, (DOCS, HD), 1)
        == 8 * lax.broadcasted_iota(jnp.int32, (DOCS, HD), 0)
    ).astype(F32)
    scores_out[...] = lax.dot_general(
        pick, totals, NT, precision=high, preferred_element_type=F32
    )

    done(kv.at[:, 0:3, 0], kx_ss)
    for i in range(4):
        msg_each(i, lambda c: c.wait_send())
    for slot in (0, 5, 6):
        q_left(slot)
    for dx in range(1, 4):
        hit_copy(dx).wait_send()
    hit_side().wait_send()

    z_each(lambda to, s: done(half(0, 0), z_ss.at[s]))

    @pl.when(zz == 1)
    def _():
        z_whole(0, 2, 1).wait_send()

    def s_done(i, _):
        s_copy(i).wait_send()
        return 0

    lax.fori_loop(0, zz + 1, s_done, 0)
    done(rs1.at[1:], r1_ss)
    done(sk_all.at[1:], ag_ss)
    done(rs2.at[1:], r2_ss)


def local(
    queries, key_heads, value_heads, out_grad, log_sums, row_delta, doc_start,
    layer_input, hash_in, hash_out, query_sketch,
):
    hbm = pl.BlockSpec(memory_space=pl.ANY)
    vmem = pl.BlockSpec(memory_space=pltpu.VMEM)
    smem = pl.BlockSpec(memory_space=pltpu.SMEM)
    dma = pltpu.SemaphoreType.DMA
    return pl.pallas_call(
        kernel,
        out_shape=(
            jax.ShapeDtypeStruct((1, 256), F32),
            jax.ShapeDtypeStruct((DOCS, 8), F32),
        ),
        in_specs=[hbm, hbm, hbm, hbm, vmem, vmem, smem, hbm, vmem, vmem, vmem],
        out_specs=(vmem, vmem),
        scratch_shapes=[
            pltpu.VMEM((2, 4, BLOCK, 512), BF16),
            pltpu.VMEM((2, 16, 2, ROWS, HD), BF16),
            pltpu.VMEM((2048, BLOCK), F32),
            pltpu.VMEM((ROWS, DIM), BF16),
            pltpu.VMEM((3, 32, HD), F32),
            pltpu.VMEM((4, 3, 8, HD), F32),
            pltpu.VMEM((K1, ROWS), BF16),
            pltpu.VMEM((4, 2, K1, ROWS), BF16),
            pltpu.VMEM((SEQ, HD), F32),
            pltpu.VMEM((K1, 2 * K2), F32),
            pltpu.VMEM((RANKS, 8, HD), F32),
            pltpu.VMEM((8, HD), F32),
            pltpu.VMEM((DOCS, 8, HD), F32),
            pltpu.VMEM((256, HD), F32),
            pltpu.VMEM((RANKS, 8, HD), F32),
            dma,
            dma((4,)), dma((4,)),
            dma, dma,
            dma((7,)), dma((4,)),
            dma((2,)), dma((4,)), dma((4,)), dma((4,)),
            dma((4,)), dma, dma, dma,
            dma, dma, dma, dma, dma, dma,
        ],
        compiler_params=pltpu.CompilerParams(
            collective_id=0, has_side_effects=True, vmem_limit_bytes=56 * 2**20
        ),
    )(
        queries, key_heads, value_heads, out_grad,
        log_sums.reshape(32, 128), row_delta.reshape(32, 128), doc_start, layer_input,
        hash_in.reshape(1, DIM), hash_out.reshape(1, HD), query_sketch,
    )


def solution(mesh):
    return jax.shard_map(
        local,
        mesh=mesh,
        in_specs=(
            P("doc", "ctx", None),
            P("doc", "ctx", None),
            P("doc", "ctx", None),
            P("doc", "ctx", None),
            P("doc", "ctx", None),
            P("doc", "ctx", None),
            P("doc"),
            P("doc", "ctx", None),
            P(),
            P("ctx"),
            P("doc", "ctx"),
        ),
        out_specs=(P("doc", "ctx"), P(None, ("doc", "ctx"))),
        check_vma=False,
    )
```

time: 94 us -> 86.1 us (0.916)
  Pallas kernels: 89.9 us -> 82 us
    pallas_call x1, Pallas kernels: 89.9 us -> 82 us  [local(): pl.pallas_call(kernel, out_shape=(jax.ShapeDtypeStruct((1, 256), F32), ja...]
where the time goes in v2:
time: 86.1 us; the launch traced here: 85.9 us
  Pallas kernels  82 us (95%)
  local copies, waits for them, and re-layouts  2.57 us (3%)
  between operations  1.29 us (1%)
    pallas_call x1, Pallas kernels, local(): pl.pallas_call(kernel, out_shape=(jax.ShapeDtypeStruct((1, 256), F32), ja...  82 us

profile of v2, /device:TPU:1, one launch (start us, length us, event | category | flops | bytes accessed | tf_op | source)
XLA Modules:
  0.0 85.9 jit_solution(755238352970692135)
XLA Ops:
  1.3 82.0 %shard_map.122 = (f32[1,256]{1,0:T(1,128)}, f32[16,8]{1,0:T(8,128)}) custom-call(bf16[1,128,4096]{2,1,0:T(8,128)(2,1)} %q_hbm.1, bf16[1,128,512]{2,1,0:T(8,128)(2,1)} %k_hbm.1, bf16[1,128,512]{2,1,0:T(8,128)(2,1)} %v_hbm.1, bf16[1,128,4096]{2,1,0:T(8,128)(2,1)} %do_hbm.1, f32[32,128]{1,0:T(8,128)} %bitcast.5, f32[32,128]{1,0:T(8,128)} %bitcast.6, ...), custom_call_target="tpu_custom_call" | custom-call | tf_op jit(solution)/shard_map/pallas_call | solution.py:426
  83.3 1.4 %copy.13 = f32[16,8]{0,1:T(8,128)} copy(f32[16,8]{1,0:T(8,128)} %get-tuple-element.3) | data formatting | bytes 1024 | tf_op jit(solution)/shard_map/pallas_call | solution.py:426
  84.7 1.2 %copy.16 = f32[1,256]{1,0:T(1,128)} copy(f32[1,256]{1,0:T(1,128)} %get-tuple-element.6) | data formatting | bytes 2048

commit v3 on v2

--- a/solution.py
+++ b/solution.py
@@ -55,16 +55,28 @@
     def done(ref, sem):
         pltpu.make_async_copy(ref, ref, sem).wait()
 
+    near_order = (4, 5, 3, 2, 6, 7, 1)
+    ctx_peers = [
+        wrap(zz + dz, 4) * 8 + wrap(in_plane + j, 8) for dz in (2, 1, 3) for j in (4, 5, 3, 2, 6, 7, 1, 0)
+    ] + [base + wrap(in_plane + j, 8) for j in near_order]
+    upper = doc // 8
+    yy = doc - 8 * upper
+    doc_peers = [(1 - upper) * 8 + wrap(yy + j, 8) for j in (4, 3, 5, 2, 6, 1, 7, 0)] + [
+        upper * 8 + wrap(yy + j, 8) for j in (4, 3, 5, 2, 6, 1, 7)
+    ]
+
     barrier = pltpu.get_barrier_semaphore()
-    for i in range(1, RANKS):
+    for peer in ctx_peers[:8]:
         pl.semaphore_signal(
-            barrier, inc=1, device_id={"ctx": wrap(me + i, RANKS)},
-            device_id_type=pl.DeviceIdType.MESH,
-        )
-    for i in range(1, DOCS):
+            barrier, inc=1, device_id={"ctx": peer}, device_id_type=pl.DeviceIdType.MESH
+        )
+    for peer in doc_peers:
         pl.semaphore_signal(
-            barrier, inc=1, device_id={"doc": wrap(doc + i, DOCS)},
-            device_id_type=pl.DeviceIdType.MESH,
+            barrier, inc=1, device_id={"doc": peer}, device_id_type=pl.DeviceIdType.MESH
+        )
+    for peer in ctx_peers[8:]:
+        pl.semaphore_signal(
+            barrier, inc=1, device_id={"ctx": peer}, device_id_type=pl.DeviceIdType.MESH
         )
     x_copy = pltpu.make_async_copy(x_hbm.at[0], xb, xsem)
     x_copy.start()
@@ -104,6 +116,10 @@
 
     z_each(z_first)
 
+    @pl.when(zz == 0)
+    def _():
+        z_first(2, 2)
+
     rows = pl.ds(pl.multiple_of(cc * ROWS, ROWS), ROWS)
 
     def q_send(slot, dx, other):
@@ -120,8 +136,14 @@
     def q_left(slot):
         done(qd.at[:, 0, 0:ROWS, :], q_ss.at[slot])
 
-    for slot, dx, other in ((0, 0, 1), (1, 1, 0), (2, 3, 0), (3, 1, 1), (4, 3, 1), (7, 0, 0)):
-        q_send(slot, dx, other)
+    def q_arrive(rb):
+        done(qd.at[:, rb], q_rs.at[rb])
+
+    near = ((1, 1, 0), (2, 3, 0), (3, 1, 1), (4, 3, 1))
+    q_send(0, 0, 1)
+    for way in near:
+        q_send(*way)
+    q_send(7, 0, 0)
 
     own_head = zz * 2 + in_plane // 4
     head_slot = in_plane - 4 * (in_plane // 4)
@@ -221,105 +243,114 @@
         rows = pl.ds(pl.multiple_of((rb * 4 + h) * HD, HD), HD)
         acc[rows, :] += r
 
-    def heads(rb, plane, chips, diagonal):
+    def attend(items, plane, chips, diagonal):
         count = chips * BLOCK
         blocks = pl.ds(plane * 4, chips)
         kk = kv[0, blocks].reshape(count, HD)
         vv = kv[1, blocks].reshape(count, HD)
         low = bias[pl.ds(pl.multiple_of(plane * PLANE, PLANE), count), :]
-        now = front(rb, 0, kk, vv)
-        for h in range(4):
-            later = front(rb, h + 1, kk, vv) if h < 3 else None
-            back(rb, h, kk, low, *now, diagonal)
+        now = front(*items[0], kk, vv)
+        for n, item in enumerate(items):
+            later = front(*items[n + 1], kk, vv) if n + 1 < len(items) else None
+            back(*item, kk, low, *now, diagonal)
             now = later
 
-    def order(i):
-        return wrap(xx + jnp.where(i == 2, 3, jnp.where(i == 3, 2, i)), 4)
-
-    def diag_step(i, _):
-        rb = order(i)
-        done(qd.at[:, rb], q_rs.at[rb])
+    own, right, left, far = xx, wrap(xx + 1, 4), wrap(xx + 3, 4), wrap(xx + 2, 4)
+
+    def diag(rb, picked):
         for r in range(4):
 
             @pl.when(rb == r)
             def _():
-                heads(r, zz, r + 1, True)
-
-        return 0
-
-    def plane_steps(plane, chips, first, last):
+                attend([(r, h) for h in picked], zz, r + 1, True)
+
+    def diag_whole(rb):
+        q_arrive(rb)
+        diag(rb, range(4))
+
+    def diag_near():
         def step(i, _):
-            heads(order(i), plane, chips, False)
+            diag_whole(jnp.where(i == 0, right, left))
             return 0
 
-        lax.fori_loop(first, last, step, 0)
+        lax.fori_loop(0, 2, step, 0)
+
+    def whole(rb, plane):
+        attend([(rb, h) for h in range(4)], plane, 4, False)
+
+    def near_heads(plane):
+        attend([(rb, h) for rb in (right, left) for h in range(4)], plane, 4, False)
+
+    early = jnp.where(zz == 3, 2, jnp.where(zz >= 1, 1, 0))
+
+    def each_early(go):
+        def step(i, _):
+            go(jnp.where(i == 0, zz - 1, 0))
+            return 0
+
+        lax.fori_loop(0, early, step, 0)
 
     for i in range(4):
         done(msg.at[i], msg_rs.at[i])
     s_arrive(zz)
 
-    lax.fori_loop(0, 1, diag_step, 0)
-
+    diag_whole(own)
     @pl.when(zz == 1)
     def _():
         done(half(0, 0), z_ss.at[0])
         z_whole(1, 3, 0).start()
 
-    for slot in (1, 2, 3, 4):
-        q_left(slot)
+    for way in near:
+        q_left(way[0])
     q_send(5, 2, 0)
     q_send(6, 2, 1)
-    lax.fori_loop(1, 3, diag_step, 0)
+    diag_near()
 
     @pl.when(zz >= 1)
     def _():
         z_arrive(zz - 1)
 
-    @pl.when(zz == 1)
-    def _():
-        z_whole(0, 2, 1).start()
-
     @pl.when(zz == 3)
     def _():
         z_arrive(0)
-
-    @pl.when(zz >= 1)
-    def _():
-        s_arrive(zz - 1)
-        plane_steps(zz - 1, 4, 0, 3)
-
-    @pl.when(zz == 3)
-    def _():
-        s_arrive(0)
-        plane_steps(0, 4, 0, 3)
-
-    lax.fori_loop(3, 4, diag_step, 0)
+        for dx in (1, 3, 2):
+            block = kv.at[:, wrap(xx + dx, 4), cc]
+            remote(block, block, z_ss.at[1], z_rs.at[0], 16 + in_plane).start()
+
+    def first_use(plane):
+        s_arrive(plane)
+        whole(own, plane)
+        near_heads(plane)
+
+    each_early(first_use)
+    diag_whole(far)
     for dx in range(1, 4):
         hit_copy(dx).start()
     pltpu.make_async_copy(hit_own, hit.at[xx, cc], hi_rs).start()
 
-    @pl.when(zz >= 1)
-    def _():
-        plane_steps(zz - 1, 4, 3, 4)
-
     @pl.when(zz == 3)
     def _():
         z_arrive(1)
-        plane_steps(0, 4, 3, 4)
-
+
+    each_early(lambda plane: whole(far, plane))
     done(hit.at[:, cc], hi_rs)
     hit_side().start()
 
-    @pl.when(zz == 3)
-    def _():
-        s_arrive(1)
-        plane_steps(1, 4, 0, 4)
-
-    @pl.when(zz == 2)
-    def _():
-        z_arrive(0)
-        s_arrive(0)
-        plane_steps(0, 4, 0, 4)
+    @pl.when(zz >= 2)
+    def _():
+        last = zz - 2
+
+        @pl.when(zz == 2)
+        def _():
+            z_arrive(0)
+
+        s_arrive(last)
+
+        def step(rb, _):
+            whole(rb, last)
+            return 0
+
+        lax.fori_loop(0, 4, step, 0)
 
     done(hit.at[:, 1 - cc], hs_rs)
     feature_bucket = lax.broadcasted_iota(jnp.int32, (K2, HD), 0).astype(F32)
@@ -343,8 +374,7 @@
         )
     part[...] = total
 
-    for i in range(1, RANKS):
-        to = wrap(me + i, RANKS)
+    for to in ctx_peers:
         rows = pl.ds(pl.multiple_of((to // 2) * 8, 8), 8)
         remote(part.at[rows, :], rs1.at[me], r1_ss, r1_rs, to).start()
     mine = pl.ds(pl.multiple_of((me // 2) * 8, 8), 8)
@@ -359,10 +389,10 @@
     sketch_out[...] = jnp.concatenate([first, second], axis=1)
     sk_send[...] = jnp.concatenate([first, second, jnp.zeros((6, HD), F32)], axis=0)
 
-    for i in range(1, DOCS):
+    for peer in doc_peers:
         pltpu.make_async_remote_copy(
             src_ref=sk_send, dst_ref=sk_all.at[doc], send_sem=ag_ss, recv_sem=ag_rs,
-            device_id={"doc": wrap(doc + i, DOCS)}, device_id_type=pl.DeviceIdType.MESH,
+            device_id={"doc": peer}, device_id_type=pl.DeviceIdType.MESH,
         ).start()
     pltpu.make_async_copy(sk_send, sk_all.at[doc], ag_rs).start()
     pltpu.make_async_copy(sk_all, sk_all, ag_rs).wait()
@@ -374,8 +404,7 @@
     odd = lax.dot_general(stored[:, HD:], flat, NT, precision=high, preferred_element_type=F32)
     part2[...] = even + pltpu.roll(odd, HD - 1, 1)
 
-    for i in range(1, RANKS):
-        to = wrap(me + i, RANKS)
+    for to in ctx_peers:
         rows = pl.ds(pl.multiple_of(to * 8, 8), 8)
         remote(part2.at[rows, :], rs2.at[me], r2_ss, r2_rs, to).start()
     mine = pl.ds(pl.multiple_of(me * 8, 8), 8)
@@ -401,9 +430,13 @@
 
     z_each(lambda to, s: done(half(0, 0), z_ss.at[s]))
 
-    @pl.when(zz == 1)
-    def _():
-        z_whole(0, 2, 1).wait_send()
+    @pl.when(zz == 0)
+    def _():
+        done(kv.at[:, 0, 0], z_ss.at[2])
+
+    @pl.when(zz == 3)
+    def _():
+        done(kv.at[:, 0:3, 0], z_ss.at[1])
 
     def s_done(i, _):
         s_copy(i).wait_send()
@@ -451,7 +484,7 @@
             dma((4,)), dma((4,)),
             dma, dma,
             dma((7,)), dma((4,)),
-            dma((2,)), dma((4,)), dma((4,)), dma((4,)),
+            dma((3,)), dma((4,)), dma((4,)), dma((4,)),
             dma((4,)), dma, dma, dma,
             dma, dma, dma, dma, dma, dma,
         ],

time: 86.1 us -> 82.6 us (0.959)
  Pallas kernels: 82 us -> 78.5 us
    pallas_call x1, Pallas kernels: 82 us -> 78.5 us  [local(): pl.pallas_call(kernel, out_shape=(jax.ShapeDtypeStruct((1, 256), F32), ja...]
where the time goes in v3:
time: 82.6 us; the launch traced here: 82.4 us
  Pallas kernels  78.5 us (95%)
  local copies, waits for them, and re-layouts  2.57 us (3%)
  between operations  1.29 us (2%)
    pallas_call x1, Pallas kernels, local(): pl.pallas_call(kernel, out_shape=(jax.ShapeDtypeStruct((1, 256), F32), ja...  78.5 us

profile of v3, /device:TPU:1, one launch (start us, length us, event | category | flops | bytes accessed | tf_op | source)
XLA Modules:
  0.0 82.4 jit_solution(5786624668265874616)
XLA Ops:
  1.3 78.5 %shard_map.122 = (f32[1,256]{1,0:T(1,128)}, f32[16,8]{1,0:T(8,128)}) custom-call(bf16[1,128,4096]{2,1,0:T(8,128)(2,1)} %q_hbm.1, bf16[1,128,512]{2,1,0:T(8,128)(2,1)} %k_hbm.1, bf16[1,128,512]{2,1,0:T(8,128)(2,1)} %v_hbm.1, bf16[1,128,4096]{2,1,0:T(8,128)(2,1)} %do_hbm.1, f32[32,128]{1,0:T(8,128)} %bitcast.5, f32[32,128]{1,0:T(8,128)} %bitcast.6, ...), custom_call_target="tpu_custom_call" | custom-call | tf_op jit(solution)/shard_map/pallas_call | solution.py:459
  79.8 1.4 %copy.13 = f32[16,8]{0,1:T(8,128)} copy(f32[16,8]{1,0:T(8,128)} %get-tuple-element.3) | data formatting | bytes 1024 | tf_op jit(solution)/shard_map/pallas_call | solution.py:459
  81.1 1.2 %copy.16 = f32[1,256]{1,0:T(1,128)} copy(f32[1,256]{1,0:T(1,128)} %get-tuple-element.6) | data formatting | bytes 2048

commit v4 on v3

--- a/solution.py
+++ b/solution.py
@@ -33,7 +33,7 @@
 def kernel(
     q_hbm, k_hbm, v_hbm, do_hbm, lse_ref, dl_ref, start_ref, x_hbm, hin_ref, hout_ref, qs_ref,
     sketch_out, scores_out,
-    qd, kv, acc, xb, ld, msg, hit_own, hit, bias, part, rs1, sk_send, sk_all, part2, rs2,
+    qd, kv, acc, xb, ld, msg, hit_own, hit, bias, part, rs1, sk_send, sk_all, part2, rs2, stage, stage_sem,
     xsem, msg_ss, msg_rs, kx_ss, kx_rs, q_ss, q_rs, z_ss, z_rs, s_ss, s_rs,
     hi_ss, hi_rs, hs_ss, hs_rs, r1_ss, r1_rs, ag_ss, ag_rs, r2_ss, r2_rs,
 ):
@@ -80,6 +80,12 @@
         )
     x_copy = pltpu.make_async_copy(x_hbm.at[0], xb, xsem)
     x_copy.start()
+    stage_copies = [
+        pltpu.make_async_copy(src.at[0], stage.at[n], stage_sem.at[n])
+        for n, src in enumerate((q_hbm, do_hbm))
+    ]
+    for copy in stage_copies:
+        copy.start()
     ld[0] = lse_ref[...] * LOG2E
     ld[1] = dl_ref[...]
     ld[2] = jnp.broadcast_to(hout_ref[...].astype(F32), (32, 128))
@@ -125,8 +131,8 @@
     def q_send(slot, dx, other):
         to = 2 * wrap(xx + dx, 4) + (1 - cc if other else cc)
         lanes = pl.ds(pl.multiple_of(to * 512, 512), 512)
-        for n, src in enumerate((q_hbm, do_hbm)):
-            src = src.at[0, :, lanes]
+        for n in range(2):
+            src = stage.at[n, :, lanes]
             dst = qd.at[n, xx, rows, :]
             if slot == 7:
                 pltpu.make_async_copy(src, dst, q_rs.at[xx]).start()
@@ -140,6 +146,8 @@
         done(qd.at[:, rb], q_rs.at[rb])
 
     near = ((1, 1, 0), (2, 3, 0), (3, 1, 1), (4, 3, 1))
+    for copy in stage_copies:
+        copy.wait()
     q_send(0, 0, 1)
     for way in near:
         q_send(*way)
@@ -480,6 +488,7 @@
             pltpu.VMEM((DOCS, 8, HD), F32),
             pltpu.VMEM((256, HD), F32),
             pltpu.VMEM((RANKS, 8, HD), F32),
+            pltpu.VMEM((2, ROWS, 4096), BF16), dma((2,)),
             dma,
             dma((4,)), dma((4,)),
             dma, dma,

time: 82.6 us -> 82.1 us (level)
  no operation moved by 1% of the time
where the time goes in v4:
time: 82.1 us; the launch traced here: 81.9 us
  Pallas kernels  78 us (95%)
  local copies, waits for them, and re-layouts  2.57 us (3%)
  between operations  1.29 us (2%)
    pallas_call x1, Pallas kernels, local(): pl.pallas_call(kernel, out_shape=(jax.ShapeDtypeStruct((1, 256), F32), ja...  78 us

profile of v4, /device:TPU:1, one launch (start us, length us, event | category | flops | bytes accessed | tf_op | source)
XLA Modules:
  0.0 81.9 jit_solution(3128715159289042621)
XLA Ops:
  1.3 78.0 %shard_map.122 = (f32[1,256]{1,0:T(1,128)}, f32[16,8]{1,0:T(8,128)}) custom-call(bf16[1,128,4096]{2,1,0:T(8,128)(2,1)} %q_hbm.1, bf16[1,128,512]{2,1,0:T(8,128)(2,1)} %k_hbm.1, bf16[1,128,512]{2,1,0:T(8,128)(2,1)} %v_hbm.1, bf16[1,128,4096]{2,1,0:T(8,128)(2,1)} %do_hbm.1, f32[32,128]{1,0:T(8,128)} %bitcast.5, f32[32,128]{1,0:T(8,128)} %bitcast.6, ...), custom_call_target="tpu_custom_call" | custom-call | tf_op jit(solution)/shard_map/pallas_call | solution.py:467
  79.3 1.4 %copy.13 = f32[16,8]{0,1:T(8,128)} copy(f32[16,8]{1,0:T(8,128)} %get-tuple-element.3) | data formatting | bytes 1024 | tf_op jit(solution)/shard_map/pallas_call | solution.py:467
  80.7 1.2 %copy.16 = f32[1,256]{1,0:T(1,128)} copy(f32[1,256]{1,0:T(1,128)} %get-tuple-element.6) | data formatting | bytes 2048
